TPU v7x, 128 devices: a whole 4x4x4 slice. The times are simulated.
128 devices in a mesh: tile: 16 (over x, y), view: 8 (over z, core).
Axes of the slice: x: 4, y: 4, z: 4, core: 2. Of those that a mesh axis runs over, the one named last changes fastest.
Arguments:
- estimate: float32 [2, 224, 448, 128], P(None, 'view', 'tile'), may hold values from 0.25 to 4
- view_data: bfloat16 [8, 16, 3, 2, 58, 58, 128], P('view', 'tile'), may hold values from 0.25 to 4
- psf: float32 [6, 3, 31], replicated, may hold values from 0 to 0.5, as said below
- background: float32 [6], replicated, may hold values from 0.1 to 1
- slot_brick: int32 [8, 16, 3], P('view', 'tile'), may hold values from 0 to 15, as said below
- slot_view: int32 [8, 16, 3], P('view', 'tile'), may hold values from 0 to 5, as said below
- intersection: int32 [8, 16, 6], P('view', 'tile'), may hold values from 0 to 1, as said below
Outputs:
- updated: float32 [2, 224, 448, 128], P(None, 'view', 'tile')
Inputs may be any that keep to these rules, and one draw needn't show every extreme that they name: `slot_brick`: within a group, the jobs are exactly the pairs (brick, view) that intersection marks, each once; every brick has at least one view and one brick of each group has all 6; the jobs of a group fill its workers' 3 slots exactly. `slot_view`: the view of each job, consistent with intersection. `intersection`: each brick's row has between 1 and 6 ones. `psf`: all taps are positive.
All inputs are finite; a program needn't handle non-finite values.
Results may differ from a plain program's by a relative error of at most 0.0003.
Values may be sent and summed in bfloat16 or wider, within the bound.
No kernel may reach another device: no remote copies, remote signals or barrier semaphores. Data moves between devices by JAX's collectives and lax.ppermute only.
A program may use at most 128 MiB of HBM per device.

v0:
```python
import jax
import jax.numpy as jnp
from jax import lax
from jax.sharding import PartitionSpec as P


def extended(array, sides, width):
    for axis, dim in sides:
        count, length = (lax.axis_size(axis), array.shape[dim])
        up = [(i, (i + 1) % count) for i in range(count - 1)]
        down = [(j, i) for i, j in up]
        last = lax.slice_in_dim(array, length - width, length, axis=dim)
        leading = lax.slice_in_dim(array, 0, width, axis=dim)
        before = lax.ppermute(last, axis, up)
        after = lax.ppermute(leading, axis, down)
        array = jnp.concatenate([before, array, after], axis=dim)
    return array


def banded(kernel_taps, order, rim_width):
    offsets = jnp.arange(order)[None, :] - jnp.arange(order)[:, None] + rim_width
    matches = offsets[:, :, None] == jnp.arange(kernel_taps.shape[0])[None, None, :]
    return jnp.sum(jnp.where(matches, kernel_taps[None, None, :], 0.0), axis=2)


def forward_blur(block, kernels, rim_width):
    band_x = banded(kernels[0], block.shape[1], rim_width)
    band_y = banded(kernels[1], block.shape[2], rim_width)
    band_z = banded(kernels[2], block.shape[3], rim_width)
    result = jnp.einsum("cxyz,wz->cxyw", block, band_z, precision=lax.Precision.HIGHEST)
    result = jnp.einsum("cxyz,vy->cxvz", result, band_y, precision=lax.Precision.HIGHEST)
    return jnp.einsum("cxyz,ux->cuyz", result, band_x, precision=lax.Precision.HIGHEST)


def backward_blur(ratio, kernels, rim_width, brick_x, brick_y):
    band_x = banded(kernels[0], ratio.shape[1], rim_width)[:, rim_width : rim_width + brick_x]
    band_y = banded(kernels[1], ratio.shape[2], rim_width)[:, rim_width : rim_width + brick_y]
    band_z = banded(kernels[2], ratio.shape[3], rim_width)
    result = jnp.einsum("cxyz,xu->cuyz", ratio, band_x, precision=lax.Precision.HIGHEST)
    result = jnp.einsum("cxyz,yv->cxvz", result, band_y, precision=lax.Precision.HIGHEST)
    return jnp.einsum("cxyz,zw->cxyw", result, band_z, precision=lax.Precision.HIGHEST)


def correction(block, measured, psf, background, view_index, rim_width, brick_x, brick_y):
    kernels = lax.dynamic_index_in_dim(psf, view_index, 0, keepdims=False)
    backdrop = lax.dynamic_index_in_dim(background, view_index, 0, keepdims=False)
    predicted = forward_blur(block, kernels, rim_width) + backdrop
    ratio = measured.astype(jnp.float32) / predicted
    return backward_blur(ratio, kernels, rim_width, brick_x, brick_y)


def on_device(estimate, view_data, psf, background, slot_brick, slot_view, intersection):
    rim_width = psf.shape[2] // 2
    channels, brick_x, brick_y, depth_cells = estimate.shape
    est_wire = estimate.astype(jnp.bfloat16)
    padded = extended(est_wire, (("tile", 2), ("view", 1)), rim_width)
    gathered = lax.all_gather(padded[None], "tile", axis=0, tiled=True)
    owners = lax.axis_size("tile")
    contrib = jnp.zeros((owners, channels, brick_x, brick_y, depth_cells), jnp.float32)
    for slot_index in range(slot_brick.shape[2]):
        brick_index = slot_brick[0, 0, slot_index]
        view_index = slot_view[0, 0, slot_index]
        block = lax.dynamic_index_in_dim(gathered, brick_index, 0, keepdims=False).astype(
            jnp.float32
        )
        factor = correction(
            block,
            view_data[0, 0, slot_index],
            psf,
            background,
            view_index,
            rim_width,
            brick_x,
            brick_y,
        )
        owner_marks = (jnp.arange(owners) == brick_index).astype(jnp.float32)
        contrib = contrib + owner_marks[:, None, None, None, None] * factor[None]
    summed = lax.psum_scatter(contrib, "tile", scatter_dimension=0, tiled=True)[0]
    views_seen = jnp.sum(intersection[0, 0]).astype(jnp.float32)
    return estimate * summed / views_seen


def solution(mesh):
    placed = (
        P(None, "view", "tile", None),
        P("view", "tile", None, None, None, None, None),
        P(),
        P(),
        P("view", "tile", None),
        P("view", "tile", None),
        P("view", "tile", None),
    )
    return jax.shard_map(
        on_device,
        mesh=mesh,
        in_specs=placed,
        out_specs=P(None, "view", "tile", None),
        check_vma=False,
    )
```

profile of v0, /device:TPU:1, one launch (start us, length us, event | category | flops | bytes accessed | tf_op | source)
XLA Modules:
  0.0 482.3 jit_solution(7533203977830049392)
XLA Ops:
  6.5 0.0 all-gather.3.cloned.1.call-start
  6.5 1.2 copy.95
  7.8 0.1 fusion.61
  7.9 4.0 collective-permute-start
  11.9 1.3 collective-permute-start.1
  13.2 2.9 collective-permute-done
  16.2 3.8 collective-permute-done.1
  20.0 0.3 pad_maximum_fusion.1
  20.3 0.0 copy-start.9
  20.3 0.0 copy-start.10
  20.3 0.0 copy-start.11
  20.4 0.0 copy-start.12
  20.4 0.1 fusion.60
  20.5 5.3 %collective-permute-start.2 = (bf16[2,15,58,128]{3,2,1,0:T(8,128)(2,1)S(1)}, bf16[2,15,58,128]{3,2,1,0:T(8,128)(2,1)S(1)}, u32[]{:S(2)}, u32[]{:S(2)}) collective-permute-start(bf16[2,15,58,128]{3,2,1,0:T(8,128)(2,1)S(1)} %get-tuple-element.17), channel_id=1, source_target_pairs={{0,1},{1,2},{2,3},{3,4},{4,5},{5,6},{6,7},{8,9},{9,10},{10,11},{11... | collective-permute-start | bytes 1336328 | tf_op jit(solution)/shard_map/ppermute | solution.py:14
  25.8 1.9 collective-permute-start.3
  27.7 3.8 collective-permute-done.2
  31.5 4.4 collective-permute-done.3
  35.9 1.8 pad_maximum_fusion
  37.7 0.0 all-gather.3.cloned.1.call-update
  37.7 0.0 all-reduce.3.cloned.1.call-start
  37.8 0.0 copy-done.9
  37.8 0.6 fusion.63
  42.0 0.0 copy-done.10
  42.0 0.6 fusion.64
  49.9 0.7 fusion.62
  50.5 1.2 compare_convert_fusion.2
  51.8 1.2 compare_convert_fusion
  53.1 2.0 select_reduce_fusion.7
  55.0 1.2 select_reduce_fusion.2
  56.3 6.5 %fusion.59 = (bf16[1,1,1,2,58,58,128]{6,3,5,4,2,1,0:T(2,128)(2,1)S(1)}, bf16[1,1,1,2,58,58,128]{6,3,5,4,2,1,0:T(2,128)(2,1)S(1)}, bf16[1,1,1,2,58,58,128]{6,3,5,4,2,1,0:T(2,128)(2,1)}) fusion(bf16[1,1,3,2,58,58,128]{6,3,5,4,2,1,0:T(2,128)(2,1)} %param.8), kind=kLoop, calls=%fused_computation.101 | loop fusion | bytes 10334208 | tf_op jit(solution)/shard_map/slice | solution.py:68
  62.8 158.6 %all-gather.3.cloned.1.call-done = bf16[32,58,58,128]{3,2,1,0:T(8,128)(2,1)} async-done(((bf16[2,58,58,128]{3,2,1,0:T(8,128)(2,1)}), bf16[32,58,58,128]{3,2,1,0:T(8,128)(2,1)}) %all-gather.3.cloned.1.call-update) | async-done | bytes 27557904 | tf_op jit(solution)/shard_map/all_gather | solution.py:57
  221.3 3.2 fusion.9
  224.6 3.7 convolution_bitcast_fusion
  228.3 5.5 %fusion = f32[58,2,58,128]{3,0,2,1:T(8,128)S(1)} fusion(f32[2,58,58,128]{3,2,1,0:T(8,128)S(1)} %convolution_bitcast_fusion, f32[58,58]{1,0:T(8,128)S(1)} %copy-done.8), kind=kOutput, calls=%fused_computation.4 | convolution fusion | flops 599384064 | bytes 6902928 | tf_op jit(solution)/shard_map/cxyz,ux->cuyz/dot_general | solution.py:32
  233.7 0.0 copy-start.3
  233.8 3.6 fusion.27
  237.4 2.0 fusion.36
  239.4 0.0 copy-done.3
  239.4 0.9 fusion.41
  240.3 0.6 copy.33
  240.9 3.2 fusion.13
  244.2 3.7 convolution_bitcast_fusion.2
  247.9 0.0 copy-done.7
  247.9 5.9 %fusion.4 = f32[58,2,58,128]{3,0,2,1:T(8,128)S(1)} fusion(f32[2,58,58,128]{3,2,1,0:T(8,128)S(1)} %convolution_bitcast_fusion.2, f32[58,58]{1,0:T(8,128)S(1)} %copy-done.7), kind=kOutput, calls=%fused_computation.8 | convolution fusion | flops 599384064 | bytes 6902928 | tf_op jit(solution)/shard_map/cxyz,ux->cuyz/dot_general | solution.py:32
  253.8 3.4 fusion.29
  257.2 2.0 fusion.30
  259.3 0.0 copy-done.2
  259.3 3.2 fusion.11
  262.5 3.8 convolution_bitcast_fusion.1
  266.4 5.5 %fusion.2 = f32[58,2,58,128]{3,0,2,1:T(8,128)S(1)} fusion(f32[2,58,58,128]{3,2,1,0:T(8,128)S(1)} %convolution_bitcast_fusion.1, f32[58,58]{1,0:T(8,128)S(1)} %copy-done.6), kind=kOutput, calls=%fused_computation.6 | convolution fusion | flops 599384064 | bytes 6902928 | tf_op jit(solution)/shard_map/cxyz,ux->cuyz/dot_general | solution.py:32
  271.9 3.4 fusion.28
  275.3 2.0 fusion.33
  277.3 0.9 fusion.44
  278.2 0.6 copy.27
  278.9 1.1 fusion.47
  280.0 0.6 copy.21
  280.6 10.7 %multiply_add_fusion = f32[16,2,28,28,128]{4,1,3,2,0:T(2,128)} fusion(f32[2,28,28,128]{3,0,2,1:T(2,128)S(1)} %copy.33, f32[2,28,28,128]{3,0,2,1:T(2,128)S(1)} %copy.27, f32[2,28,28,128]{3,0,2,1:T(2,128)S(1)} %copy.21, f32[16]{0:T(128)S(1)} %get-tuple-element.45, f32[16]{0:T(128)S(1)} %get-tuple-element.46, f32[16]{0:T(128)S(1)} %copy-done.13), kind=kLoop, calls=%fused_computation | loop fusion | flops 16056320 | bytes 15253696 | tf_op jit(solution)/shard_map/add | solution.py:77
  291.3 0.0 all-reduce.3.cloned.1.call-update
  291.3 0.6 copy-done.14
  292.0 0.6 reduce_sum.104
  293.3 0.0 copy-done.15
  293.3 0.6 dynamic-slice
  293.9 178.2 %all-reduce.3.cloned.1.call-done = f32[16,2,28,28,128]{4,1,3,2,0:T(2,128)} async-done(((f32[16,2,28,28,128]{4,1,3,2,0:T(2,128)}), f32[16,2,28,28,128]{4,1,3,2,0:T(2,128)}) %all-reduce.3.cloned.1.call-update) | async-done | bytes 12845072
  472.1 3.1 fusion.40
  (25 shorter events, 0.1 us)
Async XLA Ops:
  6.5 214.8 %all-gather.3.cloned.1.call-start = ((), (), s32[]{:S(2)}) async-start(), calls=%async_computation | async-start | bytes 32309248 | tf_op jit(solution)/shard_map/all_gather | solution.py:57
  7.9 8.3 %collective-permute-start = (bf16[2,28,15,128]{3,2,1,0:T(8,128)(2,1)S(1)}, bf16[2,28,15,128]{3,2,1,0:T(8,128)(2,1)S(1)}, u32[]{:S(2)}, u32[]{:S(2)}) collective-permute-start(bf16[2,28,15,128]{3,2,1,0:T(8,128)(2,1)S(1)} %get-tuple-element.19), channel_id=1, source_target_pairs={{0,8},{8,16},{16,24},{24,32},{32,40},{40,48},{48,56},{56,64},{64,7... | collective-permute-start | bytes 645128 | tf_op jit(solution)/shard_map/ppermute | solution.py:14
  11.9 8.0 %collective-permute-start.1 = (bf16[2,28,15,128]{3,2,1,0:T(8,128)(2,1)S(1)}, bf16[2,28,15,128]{3,2,1,0:T(8,128)(2,1)S(1)}, u32[]{:S(2)}, u32[]{:S(2)}) collective-permute-start(bf16[2,28,15,128]{3,2,1,0:T(8,128)(2,1)S(1)} %get-tuple-element.20), channel_id=1, source_target_pairs={{8,0},{16,8},{24,16},{32,24},{40,32},{48,40},{56,48},{64,56},{72,6... | collective-permute-start | bytes 645128 | tf_op jit(solution)/shard_map/ppermute | solution.py:15
  20.3 17.4 %copy-start.9 = (s32[1,1,3]{2,1,0:T(1,128)S(1)}, s32[1,1,3]{2,1,0:T(1,128)}, u32[]{:S(2)}) copy-start(s32[1,1,3]{2,1,0:T(1,128)} %param.11) | copy-start | bytes 40
  20.3 21.7 %copy-start.10 = (s32[1,1,3]{2,1,0:T(1,128)S(1)}, s32[1,1,3]{2,1,0:T(1,128)}, u32[]{:S(2)}) copy-start(s32[1,1,3]{2,1,0:T(1,128)} %param.12) | copy-start | bytes 40
  20.3 29.5 %copy-start.11 = (f32[6]{0:T(128)S(1)}, f32[6]{0:T(128)}, u32[]{:S(2)}) copy-start(f32[6]{0:T(128)} %param.10) | copy-start | bytes 76
  20.4 32.6 %copy-start.12 = (f32[6,3,31]{2,1,0:T(4,128)S(1)}, f32[6,3,31]{2,1,0:T(4,128)}, u32[]{:S(2)}) copy-start(f32[6,3,31]{2,1,0:T(4,128)} %param.9) | copy-start | bytes 6700
  20.5 11.1 %collective-permute-start.2 = (bf16[2,15,58,128]{3,2,1,0:T(8,128)(2,1)S(1)}, bf16[2,15,58,128]{3,2,1,0:T(8,128)(2,1)S(1)}, u32[]{:S(2)}, u32[]{:S(2)}) collective-permute-start(bf16[2,15,58,128]{3,2,1,0:T(8,128)(2,1)S(1)} %get-tuple-element.17), channel_id=1, source_target_pairs={{0,1},{1,2},{2,3},{3,4},{4,5},{5,6},{6,7},{8,9},{9,10},{10,11},{11... | collective-permute-start | bytes 1336328 | tf_op jit(solution)/shard_map/ppermute | solution.py:14
  25.8 10.1 %collective-permute-start.3 = (bf16[2,15,58,128]{3,2,1,0:T(8,128)(2,1)S(1)}, bf16[2,15,58,128]{3,2,1,0:T(8,128)(2,1)S(1)}, u32[]{:S(2)}, u32[]{:S(2)}) collective-permute-start(bf16[2,15,58,128]{3,2,1,0:T(8,128)(2,1)S(1)} %get-tuple-element.18), channel_id=1, source_target_pairs={{1,0},{2,1},{3,2},{4,3},{5,4},{6,5},{7,6},{9,8},{10,9},{11,10},{12... | collective-permute-start | bytes 1336328 | tf_op jit(solution)/shard_map/ppermute | solution.py:15
  37.7 434.4 %all-reduce.3.cloned.1.call-start = ((), (), s32[]{:S(2)}) async-start(), calls=%async_computation.1 | async-start | bytes 25690112
  221.3 3.3 copy-start.5
  224.6 3.7 copy-start.8
  228.3 5.5 %copy-start.1 = (bf16[1,1,1,2,58,58,128]{6,3,5,4,2,1,0:T(2,128)(2,1)S(1)}, bf16[1,1,1,2,58,58,128]{6,3,5,4,2,1,0:T(2,128)(2,1)}, u32[]{:S(2)}) copy-start(bf16[1,1,1,2,58,58,128]{6,3,5,4,2,1,0:T(2,128)(2,1)} %get-tuple-element.16) | copy-start | bytes 5167108
  233.7 5.7 %copy-start.3 = (f32[128,128]{1,0:T(8,128)S(1)}, f32[128,128]{1,0:T(8,128)}, u32[]{:S(2)}) copy-start(f32[128,128]{1,0:T(8,128)} %get-tuple-element.6) | copy-start | bytes 196612
  240.3 3.9 copy-start.4
  244.2 3.7 copy-start.7
  253.8 5.5 %copy-start.2 = (f32[128,128]{1,0:T(8,128)S(1)}, f32[128,128]{1,0:T(8,128)}, u32[]{:S(2)}) copy-start(f32[128,128]{1,0:T(8,128)} %get-tuple-element.7) | copy-start | bytes 196612
  262.5 3.9 copy-start.6
  277.3 3.3 copy-start.13
  291.3 0.7 copy-start.14
  291.3 1.9 copy-start.15
  291.3 180.8 %copy-start = (f32[2,28,28,128]{3,0,2,1:T(2,128)S(1)}, f32[2,28,28,128]{3,0,2,1:T(2,128)}, u32[]{:S(2)}) copy-start(f32[2,28,28,128]{3,0,2,1:T(2,128)} %param.7) | copy-start | bytes 2408452
Sparse Core Ops, SparseCore 0:
  37.8 183.4 all-gather.2
  291.5 180.6 all-reduce.2
where the time goes:
time: 487 us; the launch traced here: 482 us
  waiting for transfers between devices  352 us (72%)
  matrix products  57.1 us (12%)
  between operations  25.6 us (5%)
  other arithmetic  22.1 us (5%)
  local copies, waits for them, and re-layouts  13 us (3%)
  starting transfers between devices  12.6 us (3%)
    unnamed x3, waiting for transfers between devices  178 us
    all_gather x1, waiting for transfers between devices, on_device(): gathered = lax.all_gather(padded[None], 'tile', axis=0, tiled=True)  159 us
    dot_general x3, matrix products, forward_blur(): jnp.einsum('cxyz,ux->cuyz', result, band_x, precision=lax.Precision.HIGHEST)  16.8 us
    dot_general x3, matrix products, forward_blur(): jnp.einsum('cxyz,vy->cxvz', result, band_y, precision=lax.Precision.HIGHEST)  11.1 us
    add x1, other arithmetic, on_device(): contrib = contrib + owner_marks[:, None, None, None, None] * factor[None]  10.7 us
    dot_general x3, matrix products, backward_blur(): jnp.einsum('cxyz,xu->cuyz', ratio, band_x, precision=lax.Precision.HIGHEST)  10.5 us
  transfers between devices with their start and end apart: 6, of which 6 were waited for; matrix products, arithmetic and copies ran while one was open for 3% of the time, Pallas kernels for 0%

commit v1 on v0

--- a/solution.py
+++ b/solution.py
@@ -54,7 +54,13 @@
     channels, brick_x, brick_y, depth_cells = estimate.shape
     est_wire = estimate.astype(jnp.bfloat16)
     padded = extended(est_wire, (("tile", 2), ("view", 1)), rim_width)
-    gathered = lax.all_gather(padded[None], "tile", axis=0, tiled=True)
+
+    def unit_use(piece_in, shard_axis, at_axis):
+        v_now = jnp.stack([piece_in for _ in range(lax.axis_size(shard_axis))])
+        f_now = lax.all_to_all(v_now, axis_name=shard_axis, split_axis=0, concat_axis=0)
+        return jnp.concatenate(f_now, axis=at_axis)
+
+    gathered = unit_use(padded[None], "tile", 0)
     owners = lax.axis_size("tile")
     contrib = jnp.zeros((owners, channels, brick_x, brick_y, depth_cells), jnp.float32)
     for slot_index in range(slot_brick.shape[2]):

time: 487 us -> 874 us (1.79)
  waiting for transfers between devices: 352 us -> 686 us
  other arithmetic: 22.1 us -> 44.8 us
  local copies, waits for them, and re-layouts: 13 us -> 35.3 us
  starting transfers between devices: 12.6 us -> 23.8 us
    all_to_all x0 -> x1, waiting for transfers between devices: none -> 467 us  [unit_use(): lax.all_to_all(v_now, axis_name=shard_axis, split_axis=0, concat_axis=0)]
    all_gather x1 -> x0, waiting for transfers between devices: 159 us -> none  [on_device(): gathered = lax.all_gather(padded[None], 'tile', axis=0, tiled=True)]
    unnamed x3 -> x2, waiting for transfers between devices: 178 us -> 211 us
    concatenate x2, other arithmetic: 2.09 us -> 23.3 us  [extended(): array = jnp.concatenate([before, array, after], axis=dim)]
    another operation x0 -> x1, local copies, waits for them, and re-layouts: none -> 16.5 us  [unit_use(): v_now = jnp.stack([piece_in for _ in range(lax.axis_size(shard_axis))])]
    all_to_all x0 -> x1, starting transfers between devices: none -> 9.89 us  [unit_use(): lax.all_to_all(v_now, axis_name=shard_axis, split_axis=0, concat_axis=0)]
  transfers between devices with their start and end apart: 6 -> 6, of which waited for: 6 -> 6; matrix products, arithmetic and copies ran while one was open for 3% -> 2% of each run, Pallas kernels for 0% -> 0%
where the time goes in v1:
time: 874 us; the launch traced here: 867 us
  waiting for transfers between devices  686 us (78%)
  matrix products  50.8 us (6%)
  other arithmetic  44.8 us (5%)
  local copies, waits for them, and re-layouts  35.3 us (4%)
  between operations  26.1 us (3%)
  starting transfers between devices  23.8 us (3%)
    all_to_all x1, waiting for transfers between devices, unit_use(): lax.all_to_all(v_now, axis_name=shard_axis, split_axis=0, concat_axis=0)  467 us
    unnamed x2, waiting for transfers between devices  211 us
    concatenate x2, other arithmetic, extended(): array = jnp.concatenate([before, array, after], axis=dim)  23.3 us
  transfers between devices with their start and end apart: 6, of which 6 were waited for; matrix products, arithmetic and copies ran while one was open for 2% of the time, Pallas kernels for 0%

profile of v1, /device:TPU:1, one launch (start us, length us, event | category | flops | bytes accessed | tf_op | source)
XLA Modules:
  0.0 867.1 jit_solution(2384236197969427295)
XLA Ops:
  6.5 1.4 convert_element_type.51
  8.0 0.3 fusion.58
  8.3 1.3 collective-permute-start.1
  9.6 4.7 collective-permute-start
  14.2 2.7 collective-permute-done.1
  16.9 0.9 collective-permute-done
  17.8 1.2 pad_maximum_fusion.1
  19.0 0.6 fusion.57
  19.6 3.9 collective-permute-start.3
  23.4 3.6 collective-permute-start.2
  27.0 4.1 collective-permute-done.3
  31.1 1.2 collective-permute-done.2
  32.3 22.1 %pad_maximum_fusion = bf16[2,58,58,128]{3,0,2,1:T(2,128)(2,1)S(1)} fusion(bf16[2,15,58,128]{3,0,2,1:T(2,128)(2,1)S(1)} %collective-permute-done.3, bf16[2,28,15,128]{3,0,2,1:T(2,128)(2,1)S(1)} %collective-permute-done.1, bf16[2,28,28,128]{3,0,2,1:T(2,128)(2,1)S(1)} %convert_element_type.51, bf16[2,28,15,128]{3,0,2,1:T(2,128)(2,1)S(1)} %collective-permute-done, ...), kind=kLoop, calls=%fused_computation.41 | loop fusion | flops 3444736 | bytes 3444736 | tf_op jit(solution)/shard_map/concatenate | solution.py:16
  54.4 16.5 %stack.3 = bf16[16,1,2,58,58,128]{5,2,4,3,1,0:T(2,128)(2,1)} broadcast(bf16[2,58,58,128]{3,0,2,1:T(2,128)(2,1)S(1)} %pad_maximum_fusion), dimensions={2,3,4,5} | broadcast | bytes 29280256 | tf_op jit(solution)/shard_map/stack | solution.py:59
  70.9 0.0 copy-start.12
  70.9 9.9 %all-to-all-start = ((bf16[16,1,2,58,58,128]{5,2,4,3,1,0:T(2,128)(2,1)}), bf16[16,1,2,58,58,128]{5,2,4,3,1,0:T(2,128)(2,1)}, u32[]{:S(2)}, u32[]{:S(2)}) async-start(bf16[16,1,2,58,58,128]{5,2,4,3,1,0:T(2,128)(2,1)} %stack.3), calls=%async_computation | async-start | bytes 55115776 | tf_op jit(solution)/shard_map/all_to_all | solution.py:60
  80.8 0.5 all-reduce.3.cloned.1.call-start
  81.3 0.0 copy-done.9
  81.4 0.6 fusion.60
  85.9 0.6 fusion.61
  94.0 0.7 fusion.59
  94.7 1.2 compare_convert_fusion.2
  95.9 1.3 compare_convert_fusion
  97.2 0.0 copy-done.12
  97.3 1.9 select_reduce_fusion.7
  99.2 1.2 select_reduce_fusion.2
  100.4 6.3 fusion.56
  106.7 466.9 %all-to-all-done = bf16[16,1,2,58,58,128]{5,2,4,3,1,0:T(2,128)(2,1)} async-done(((bf16[16,1,2,58,58,128]{5,2,4,3,1,0:T(2,128)(2,1)}), bf16[16,1,2,58,58,128]{5,2,4,3,1,0:T(2,128)(2,1)}, u32[]{:S(2)}, u32[]{:S(2)}) %all-to-all-start) | async-done | bytes 27557920 | tf_op jit(solution)/shard_map/all_to_all | solution.py:60
  573.7 6.1 constant_dynamic-slice_fusion.4
  579.8 1.7 fusion.9
  581.5 0.0 copy-done.5
  581.5 0.0 copy-start.8
  581.5 3.6 convolution_bitcast_fusion
  585.1 0.0 copy-done.8
  585.1 0.0 copy-start.1
  585.2 5.6 fusion
  590.8 0.0 copy-done.1
  590.8 3.3 fusion.27
  594.1 2.0 fusion.36
  596.1 0.9 fusion.41
  597.0 0.6 copy.35
  597.6 1.7 fusion.11
  599.4 3.8 convolution_bitcast_fusion.1
  603.2 0.0 copy-done.7
  603.2 5.2 fusion.2
  608.5 3.2 fusion.28
  611.7 2.0 fusion.33
  613.8 0.9 fusion.44
  614.6 1.0 copy.28
  615.7 1.7 fusion.13
  617.4 3.4 convolution_bitcast_fusion.2
  620.8 5.2 fusion.4
  626.0 3.6 fusion.29
  629.6 2.0 fusion.30
  631.7 0.9 fusion.47
  632.5 0.6 copy.21
  633.2 0.0 copy-done.13
  633.2 10.7 %multiply_add_fusion = f32[16,2,28,28,128]{4,1,3,2,0:T(2,128)} fusion(f32[2,28,28,128]{3,0,2,1:T(2,128)S(1)} %copy.35, f32[2,28,28,128]{3,0,2,1:T(2,128)S(1)} %copy.28, f32[2,28,28,128]{3,0,2,1:T(2,128)S(1)} %copy.21, f32[16]{0:T(128)S(1)} %get-tuple-element.48, f32[16]{0:T(128)S(1)} %get-tuple-element.49, f32[16]{0:T(128)S(1)} %copy-done.13), kind=kLoop, calls=%fused_computation | loop fusion | flops 16056320 | bytes 15253696 | tf_op jit(solution)/shard_map/add | solution.py:83
  643.9 0.0 all-reduce.3.cloned.1.call-update
  643.9 0.6 copy-done.14
  644.5 0.6 reduce_sum.104
  645.8 0.6 dynamic-slice.3
  646.4 210.6 %all-reduce.3.cloned.1.call-done = f32[16,2,28,28,128]{4,1,3,2,0:T(2,128)} async-done(((f32[16,2,28,28,128]{4,1,3,2,0:T(2,128)}), f32[16,2,28,28,128]{4,1,3,2,0:T(2,128)}) %all-reduce.3.cloned.1.call-update) | async-done | bytes 12845072
  857.0 3.1 fusion.40
  (26 shorter events, 0.1 us)
Async XLA Ops:
  8.3 8.6 collective-permute-start.1
  9.6 8.2 collective-permute-start
  19.6 11.6 %collective-permute-start.3 = (bf16[2,15,58,128]{3,0,2,1:T(2,128)(2,1)S(1)}, bf16[2,15,58,128]{3,0,2,1:T(2,128)(2,1)S(1)}, u32[]{:S(2)}, u32[]{:S(2)}) collective-permute-start(bf16[2,15,58,128]{3,0,2,1:T(2,128)(2,1)S(1)} %get-tuple-element.21), channel_id=1, source_target_pairs={{1,0},{2,1},{3,2},{4,3},{5,4},{6,5},{7,6},{9,8},{10,9},{11,10},{12... | collective-permute-start | bytes 1336328 | tf_op jit(solution)/shard_map/ppermute | solution.py:15
  23.4 8.9 %collective-permute-start.2 = (bf16[2,15,58,128]{3,0,2,1:T(2,128)(2,1)S(1)}, bf16[2,15,58,128]{3,0,2,1:T(2,128)(2,1)S(1)}, u32[]{:S(2)}, u32[]{:S(2)}) collective-permute-start(bf16[2,15,58,128]{3,0,2,1:T(2,128)(2,1)S(1)} %get-tuple-element.20), channel_id=1, source_target_pairs={{0,1},{1,2},{2,3},{3,4},{4,5},{5,6},{6,7},{8,9},{9,10},{10,11},{11... | collective-permute-start | bytes 1336328 | tf_op jit(solution)/shard_map/ppermute | solution.py:14
  70.9 10.4 %copy-start.9 = (s32[1,1,3]{2,1,0:T(1,128)S(1)}, s32[1,1,3]{2,1,0:T(1,128)}, u32[]{:S(2)}) copy-start(s32[1,1,3]{2,1,0:T(1,128)} %param.11) | copy-start | bytes 40
  70.9 15.0 %copy-start.10 = (s32[1,1,3]{2,1,0:T(1,128)S(1)}, s32[1,1,3]{2,1,0:T(1,128)}, u32[]{:S(2)}) copy-start(s32[1,1,3]{2,1,0:T(1,128)} %param.12) | copy-start | bytes 40
  70.9 23.1 %copy-start.11 = (f32[6]{0:T(128)S(1)}, f32[6]{0:T(128)}, u32[]{:S(2)}) copy-start(f32[6]{0:T(128)} %param.10) | copy-start | bytes 76
  70.9 26.3 %copy-start.12 = (f32[6,3,31]{2,1,0:T(4,128)S(1)}, f32[6,3,31]{2,1,0:T(4,128)}, u32[]{:S(2)}) copy-start(f32[6,3,31]{2,1,0:T(4,128)} %param.9) | copy-start | bytes 6700
  70.9 502.7 %all-to-all-start = ((bf16[16,1,2,58,58,128]{5,2,4,3,1,0:T(2,128)(2,1)}), bf16[16,1,2,58,58,128]{5,2,4,3,1,0:T(2,128)(2,1)}, u32[]{:S(2)}, u32[]{:S(2)}) async-start(bf16[16,1,2,58,58,128]{5,2,4,3,1,0:T(2,128)(2,1)} %stack.3), calls=%async_computation | async-start | bytes 55115776 | tf_op jit(solution)/shard_map/all_to_all | solution.py:60
  80.8 776.2 %all-reduce.3.cloned.1.call-start = ((), (), s32[]{:S(2)}) async-start(), calls=%async_computation.1 | async-start | bytes 25690112
  573.7 6.1 copy-start.3
  579.7 1.8 copy-start.5
  581.5 3.6 copy-start.8
  585.1 5.6 copy-start.1
  594.1 3.6 copy-start.2
  597.0 2.4 copy-start.4
  599.4 3.9 copy-start.7
  617.3 3.4 copy-start.6
  629.6 3.6 copy-start.13
  643.9 0.7 copy-start.14
  643.9 1.9 copy-start.15
  643.9 213.1 %copy-start = (f32[2,28,28,128]{3,0,2,1:T(2,128)S(1)}, f32[2,28,28,128]{3,0,2,1:T(2,128)}, u32[]{:S(2)}) copy-start(f32[2,28,28,128]{3,0,2,1:T(2,128)} %param.7) | copy-start | bytes 2408452
Sparse Core Ops, SparseCore 0:
  644.0 212.9 all-reduce.2
